TPU v7x, 256 devices: a whole 4x4x8 slice. The times are simulated.
256 devices in a mesh: ka: 4 (over z_hi, core), fit: 64 (over x, y, z_lo).
Axes of the slice: x: 4, y: 4, z: 8 (z_hi: 2, z_lo: 4; z = z_hi * 4 + z_lo), core: 2. Of those that a mesh axis runs over, the one named last changes fastest.
Arguments:
- integrals: bfloat16 [3, 4, 64, 48, 64, 128], P(None, 'ka', 'fit'), may hold values from -0.3125 to 0.3125
- block_lists: int32 [3, 4, 64, 2, 48], P(None, 'ka', 'fit'), may hold values from 0 to 15, as said below
- coeff: bfloat16 [4, 2, 1024, 256], P('ka', None, 'fit'), may hold values from -6 to 6
- match: int32 [3, 4], replicated, may hold values from 0 to 3, each once within a row
- ex_blocks: int32 [4, 2, 64], P('ka'), may hold values from 0 to 15, as said below
Outputs:
- exchange: float32 [4, 4096, 128], P('ka', 'fit')
Inputs may be any that keep to these rules, and one draw needn't show every extreme that they name: `block_lists`: each integral matrix lists 48 distinct blocks; each entry is a block index below 16, row first then column. `ex_blocks`: each k-point lists 64 distinct blocks, none on the diagonal (row block differs from column block).
All inputs are finite; a program needn't handle non-finite values.
Results may differ from a plain program's by a relative error of at most 0.0036.
Values may be sent and summed in bfloat16 or wider, within the bound.
A program may use at most 128 MiB of HBM per device.

v0:
```python
import jax
import jax.numpy as jnp
from jax import lax
from jax.sharding import PartitionSpec as P


def block_operands(coeff_one, edge):
    nblocks = coeff_one.shape[1] // edge
    real = coeff_one[0].reshape(nblocks, edge, -1)
    imag = coeff_one[1].reshape(nblocks, edge, -1)
    upper = jnp.concatenate([real, imag], axis=2)
    lower = jnp.concatenate([-imag, real], axis=2)
    return jnp.concatenate([upper, lower], axis=1)


def half_transform(lmat, lists, operands):
    nblocks = operands.shape[0]
    picked = jnp.take(operands, lists[1], axis=0)
    prods = jnp.einsum("bmi,bij->bmj", lmat, picked, preferred_element_type=jnp.float32)
    onehot = (lists[0][None, :] == jnp.arange(nblocks, dtype=jnp.int32)[:, None]).astype(
        jnp.float32
    )
    rows = jnp.einsum("rb,bmj->rmj", onehot, prods, precision=lax.Precision.HIGHEST)
    return rows.astype(jnp.bfloat16)


def exchange_blocks(xmat, listed):
    occ = xmat.shape[2] // 2
    left = jnp.take(xmat, listed[0], axis=0)
    right = jnp.take(xmat, listed[1], axis=0)
    swapped = jnp.concatenate([left[:, :, occ:], -left[:, :, :occ]], axis=2)
    kreal = jnp.einsum("emj,enj->emn", left, right, preferred_element_type=jnp.float32)
    kimag = jnp.einsum("emj,enj->emn", swapped, right, preferred_element_type=jnp.float32)
    return jnp.concatenate([kreal, kimag], axis=2)


def on_device(integrals, block_lists, coeff, match, ex_blocks):
    kdev = coeff.shape[0]
    nq = integrals.shape[0]
    adev = integrals.shape[2]
    edge = integrals.shape[4]
    occ = coeff.shape[3]
    nexch = ex_blocks.shape[2]
    naux = adev * lax.axis_size("fit")
    factor = -((nq * naux * occ) ** (-0.5))
    kglob = lax.axis_index("ka") * kdev + jnp.arange(kdev, dtype=jnp.int32)
    shards = lax.all_gather(coeff, "ka", axis=0, tiled=True)
    pending = jnp.zeros((kdev, nexch * edge, 2 * edge), jnp.float32)
    total = None
    for qq in range(nq):
        partner = jnp.take(match[qq], kglob, axis=0)
        partner_full = lax.all_gather(jnp.take(shards, partner, axis=0), "fit", axis=2, tiled=True)
        operands = block_operands(partner_full[0], edge)
        xmat = half_transform(integrals[qq, 0, 0], block_lists[qq, 0, 0], operands)
        summed = exchange_blocks(xmat, ex_blocks[0])
        blocks_all = [summed]
        flat = (jnp.stack(blocks_all) * factor).reshape(kdev, nexch * edge, 2 * edge)
        pending = pending + flat
    whole = lax.psum(pending, "fit")
    share = whole.shape[1] // lax.axis_size("fit")
    total = lax.dynamic_slice_in_dim(whole, lax.axis_index("fit") * share, share, 1)
    return total


def solution(mesh):
    return jax.shard_map(
        on_device,
        mesh=mesh,
        in_specs=(
            P(None, "ka", "fit", None, None, None),
            P(None, "ka", "fit", None, None),
            P("ka", None, "fit", None),
            P(),
            P("ka", None, None),
        ),
        out_specs=P("ka", "fit", None),
        check_vma=False,
    )
```

profile of v0, /device:TPU:94, one launch (start us, length us, event | category | flops | bytes accessed | tf_op | source)
XLA Modules:
  0.0 1852.3 jit_solution(7708082397937562943)
XLA Ops:
  6.5 0.8 fusion.86
  7.3 0.7 fusion.87
  11.9 0.6 fusion.89
  14.4 9.4 all_gather.12
  23.7 0.6 dynamic-slice_select_fusion
  24.4 0.7 all-gather.4.cloned.1.call-update
  25.2 0.7 all-gather.8.cloned.1.call-update
  25.9 0.7 compare_and_fusion
  26.6 0.7 slice_bitcast_fusion
  27.4 0.8 compare_and_fusion.2
  28.2 346.1 %all-gather.6.cloned.1.call-done = bf16[1,2,1024,256]{3,2,1,0:T(8,128)(2,1)} async-done(((bf16[1,2,16,256]{3,2,1,0:T(8,128)(2,1)}), bf16[1,2,1024,256]{3,2,1,0:T(8,128)(2,1)}) %all-gather.6.cloned.1.call-update) | async-done | bytes 1048592 | tf_op jit(solution)/shard_map/all_gather | solution.py:52
  374.3 1.3 fusion.84
  375.9 4.9 gather_fusion.3
  380.8 4.3 fusion.33
  385.1 5.7 fusion.47
  390.9 0.6 copy.28
  391.5 330.7 %all-gather.4.cloned.1.call-done = bf16[1,2,1024,256]{3,2,1,0:T(8,128)(2,1)} async-done(((bf16[1,2,16,256]{3,2,1,0:T(8,128)(2,1)}), bf16[1,2,1024,256]{3,2,1,0:T(8,128)(2,1)}) %all-gather.4.cloned.1.call-update) | async-done | bytes 1048592 | tf_op jit(solution)/shard_map/all_gather | solution.py:52
  722.2 1.3 fusion.85
  723.8 5.4 gather_fusion
  729.1 4.3 fusion.30
  733.5 5.7 fusion.44
  739.2 0.6 copy.25
  739.8 2.8 gather_fusion.4
  742.6 2.8 gather_fusion.1
  745.4 2.9 gather_fusion.2
  748.3 2.9 gather_fusion.5
  751.2 318.9 %all-gather.8.cloned.1.call-done = bf16[1,2,1024,256]{3,2,1,0:T(8,128)(2,1)} async-done(((bf16[1,2,16,256]{3,2,1,0:T(8,128)(2,1)}), bf16[1,2,1024,256]{3,2,1,0:T(8,128)(2,1)}) %all-gather.8.cloned.1.call-update) | async-done | bytes 1048592 | tf_op jit(solution)/shard_map/all_gather | solution.py:52
  1070.1 1.3 fusion.83
  1071.7 5.1 gather_fusion.6
  1076.8 4.3 fusion.36
  1081.1 5.7 fusion.50
  1087.4 2.9 gather_fusion.7
  1090.3 2.8 gather_fusion.8
  1093.1 5.5 broadcast_select_fusion.3
  1098.6 2.3 fusion.82
  1101.1 1.9 copy-done.1
  1103.0 1.3 fusion.41
  1104.4 0.9 copy-done
  1105.2 1.3 fusion.42
  1106.6 2.4 fusion.80
  1109.0 1.3 copy-done.2
  1110.2 1.3 fusion.43
  1111.6 3.1 fusion.15
  1114.7 1.6 fusion.19
  1116.4 3.1 fusion.23
  1119.5 3.0 fusion.40
  1122.6 721.6 %all-reduce.2.cloned.1.call-done = f32[1,4096,128]{2,1,0:T(8,128)} async-done(((f32[1,4096,128]{2,1,0:T(8,128)}), f32[1,4096,128]{2,1,0:T(8,128)}) %all-reduce.2.cloned.1.call-update) | async-done | bytes 2097168 | tf_op jit(solution)/shard_map/psum | solution.py:59
  1844.1 1.4 constant_dynamic-slice_fusion.3
  (20 shorter events, 1.9 us)
Async XLA Ops:
  6.5 367.8 %all-gather.6.cloned.1.call-start = ((), (), s32[]{:S(2)}) async-start(), calls=%async_computation.1 | async-start | bytes 1064960 | tf_op jit(solution)/shard_map/all_gather | solution.py:52
  24.4 697.8 %all-gather.4.cloned.1.call-start = ((), (), s32[]{:S(2)}) async-start(), calls=%async_computation | async-start | bytes 1064960 | tf_op jit(solution)/shard_map/all_gather | solution.py:52
  25.1 1045.0 %all-gather.8.cloned.1.call-start = ((), (), s32[]{:S(2)}) async-start(), calls=%async_computation.2 | async-start | bytes 1064960 | tf_op jit(solution)/shard_map/all_gather | solution.py:52
  25.9 1818.3 %all-reduce.2.cloned.1.call-start = ((), (), s32[]{:S(2)}) async-start(), calls=%async_computation.3 | async-start | bytes 4194304 | tf_op jit(solution)/shard_map/psum | solution.py:59
  1100.8 2.2 copy-start.1
  1103.0 2.2 copy-start
  1106.5 3.7 copy-start.2
Sparse Core Ops, SparseCore 0:
  24.5 349.7 all-gather.5
  376.1 346.0 all-gather.3
  724.0 346.0 all-gather.7
  1122.7 721.4 all-reduce.1
where the time goes:
time: 1860 us; the launch traced here: 1850 us
  waiting for transfers between devices  1720 us (92%)
  local copies, waits for them, and re-layouts  44.9 us (2%)
  matrix products  42.1 us (2%)
  between operations  19.3 us (1%)
    all_gather x3, waiting for transfers between devices, on_device(): lax.all_gather(jnp.take(shards, partner, axis=0), 'fit', axis=2, tiled=True)  996 us
    psum x1, waiting for transfers between devices, on_device(): whole = lax.psum(pending, 'fit')  722 us
  transfers between devices with their start and end apart: 4, of which 4 were waited for; matrix products, arithmetic and copies ran while one was open for 3% of the time, Pallas kernels for 0%

commit v1 on v0

--- a/solution.py
+++ b/solution.py
@@ -49,7 +49,12 @@
     total = None
     for qq in range(nq):
         partner = jnp.take(match[qq], kglob, axis=0)
-        partner_full = lax.all_gather(jnp.take(shards, partner, axis=0), "fit", axis=2, tiled=True)
+        partner_full = jnp.concatenate(
+            lax.all_to_all(
+                jnp.stack([jnp.take(shards, partner, axis=0)] * lax.axis_size("fit")), "fit", 0, 0
+            ),
+            axis=2,
+        )
         operands = block_operands(partner_full[0], edge)
         xmat = half_transform(integrals[qq, 0, 0], block_lists[qq, 0, 0], operands)
         summed = exchange_blocks(xmat, ex_blocks[0])

time: 1860 us -> 933 us (0.50)
  waiting for transfers between devices: 1720 us -> 741 us
  blocking collectives: 9.37 us -> 44.3 us
  starting transfers between devices: 0.12 us -> 22.3 us
    all_gather x3 -> x0, waiting for transfers between devices: 996 us -> none  [on_device(): lax.all_gather(jnp.take(shards, partner, axis=0), 'fit', axis=2, tiled=True)]
    all_to_all x0 -> x1, blocking collectives: none -> 35 us  [on_device(): lax.all_to_all(jnp.stack([jnp.take(shards, partner, axis=0)] * lax.axis_s...]
    all_to_all x0 -> x2, starting transfers between devices: none -> 21.9 us  [on_device(): lax.all_to_all(jnp.stack([jnp.take(shards, partner, axis=0)] * lax.axis_s...]
  transfers between devices with their start and end apart: 4 -> 3, of which waited for: 4 -> 2; matrix products, arithmetic and copies ran while one was open for 3% -> 5% of each run, Pallas kernels for 0% -> 0%
where the time goes in v1:
time: 933 us; the launch traced here: 929 us
  waiting for transfers between devices  741 us (79%)
  blocking collectives  44.3 us (5%)
  local copies, waits for them, and re-layouts  44 us (5%)
  matrix products  42.1 us (5%)
  starting transfers between devices  22.3 us (2%)
  between operations  19.4 us (2%)
  other arithmetic  15.6 us (2%)
    psum x1, waiting for transfers between devices, on_device(): whole = lax.psum(pending, 'fit')  723 us
    all_to_all x1, blocking collectives, on_device(): lax.all_to_all(jnp.stack([jnp.take(shards, partner, axis=0)] * lax.axis_s...  35 us
    all_to_all x2, starting transfers between devices, on_device(): lax.all_to_all(jnp.stack([jnp.take(shards, partner, axis=0)] * lax.axis_s...  21.9 us
  transfers between devices with their start and end apart: 3, of which 2 were waited for; matrix products, arithmetic and copies ran while one was open for 5% of the time, Pallas kernels for 0%

profile of v1, /device:TPU:94, one launch (start us, length us, event | category | flops | bytes accessed | tf_op | source)
XLA Modules:
  0.0 928.6 jit_solution(14827733496726697841)
XLA Ops:
  6.5 0.8 fusion.86
  7.3 0.6 fusion.89
  9.6 0.7 fusion.87
  14.0 9.4 %all_gather.3 = bf16[4,2,16,256]{3,2,1,0:T(8,128)(2,1)S(1)} all-gather(bf16[1,2,16,256]{3,2,1,0:T(8,128)(2,1)} %param.13), channel_id=1, replica_groups=mesh['ka'=4,'fit'=64] {'ka'}, dimensions={0}, use_global_device_ids=true | all-gather | bytes 81920 | tf_op jit(solution)/shard_map/all_gather | solution.py:47
  23.5 35.0 %all_to_all.15 = bf16[64,1,2,16,256]{4,3,2,1,0:T(8,128)(2,1)S(1)} all-to-all(bf16[64,1,2,16,256]{4,3,2,1,0:T(8,128)(2,1)S(1)} %stack.7), channel_id=1, replica_groups=mesh['ka'=4,'fit'=64] {'fit'}, dimensions={0} | all-to-all | bytes 2097152 | tf_op jit(solution)/shard_map/all_to_all | solution.py:53
  58.5 1.1 stack.8
  59.6 10.6 %all-to-all-start.2 = ((bf16[64,1,2,16,256]{4,3,2,1,0:T(8,128)(2,1)}), bf16[64,1,2,16,256]{4,3,2,1,0:T(8,128)(2,1)S(1)}, u32[]{:S(2)}, u32[]{:S(2)}) async-start(bf16[64,1,2,16,256]{4,3,2,1,0:T(8,128)(2,1)} %stack.8), calls=%async_computation.2 | async-start | bytes 2097152 | tf_op jit(solution)/shard_map/all_to_all | solution.py:53
  70.5 0.2 maximum_maximum_fusion.1
  70.7 5.0 gather_fusion.3
  75.6 17.6 %all-to-all-done.2 = bf16[64,1,2,16,256]{4,3,2,1,0:T(8,128)(2,1)S(1)} async-done(((bf16[64,1,2,16,256]{4,3,2,1,0:T(8,128)(2,1)}), bf16[64,1,2,16,256]{4,3,2,1,0:T(8,128)(2,1)S(1)}, u32[]{:S(2)}, u32[]{:S(2)}) %all-to-all-start.2) | async-done | bytes 1048608 | tf_op jit(solution)/shard_map/all_to_all | solution.py:53
  93.2 1.1 stack.6
  94.3 11.4 %all-to-all-start = ((bf16[64,1,2,16,256]{4,3,2,1,0:T(8,128)(2,1)}), bf16[64,1,2,16,256]{4,3,2,1,0:T(8,128)(2,1)}, u32[]{:S(2)}, u32[]{:S(2)}) async-start(bf16[64,1,2,16,256]{4,3,2,1,0:T(8,128)(2,1)} %stack.6), calls=%async_computation | async-start | bytes 2097152 | tf_op jit(solution)/shard_map/all_to_all | solution.py:53
  105.7 0.3 all-reduce.2.cloned.1.call-start
  106.1 4.3 fusion.33
  110.4 5.7 fusion.47
  116.1 0.6 copy.28
  116.9 0.2 maximum_maximum_fusion.2
  117.1 5.5 gather_fusion.6
  122.6 4.3 fusion.36
  126.9 5.7 fusion.50
  132.6 0.6 copy.31
  133.2 2.8 gather_fusion.4
  136.0 2.8 gather_fusion.7
  138.8 2.8 gather_fusion.8
  141.6 2.8 gather_fusion.5
  144.4 1.3 fusion.85
  145.9 5.1 gather_fusion
  151.1 4.3 fusion.30
  155.4 5.7 fusion.44
  161.1 0.6 copy.25
  161.7 2.8 gather_fusion.1
  164.5 2.8 gather_fusion.2
  167.3 5.5 broadcast_select_fusion.3
  172.8 2.3 fusion.80
  175.1 0.3 fusion.81
  175.4 1.9 copy-done.1
  177.3 1.3 fusion.43
  178.6 0.9 copy-done
  179.5 1.3 fusion.42
  180.8 2.4 fusion.82
  183.2 1.3 copy-done.2
  184.5 1.3 fusion.41
  185.8 3.1 fusion.23
  189.0 1.6 fusion.19
  190.6 3.1 fusion.15
  193.8 3.0 fusion.40
  196.8 723.3 %all-reduce.2.cloned.1.call-done = f32[1,4096,128]{2,1,0:T(8,128)} async-done(((f32[1,4096,128]{2,1,0:T(8,128)}), f32[1,4096,128]{2,1,0:T(8,128)}) %all-reduce.2.cloned.1.call-update) | async-done | bytes 2097168 | tf_op jit(solution)/shard_map/psum | solution.py:64
  920.1 1.4 constant_dynamic-slice_fusion.3
  (23 shorter events, 0.8 us)
Async XLA Ops:
  6.5 63.7 %copy-start.3 = (s32[3,1,1,2,48]{4,3,2,1,0:T(2,128)S(1)}, s32[3,1,1,2,48]{4,3,2,1,0:T(2,128)}, u32[]{:S(2)}) copy-start(s32[3,1,1,2,48]{4,3,2,1,0:T(2,128)} %param.12) | copy-start | bytes 3460
  6.5 63.7 %copy-start.4 = (s32[1,2,64]{2,1,0:T(2,128)S(1)}, s32[1,2,64]{2,1,0:T(2,128)}, u32[]{:S(2)}) copy-start(s32[1,2,64]{2,1,0:T(2,128)} %param.15) | copy-start | bytes 1540
  59.6 33.6 %all-to-all-start.2 = ((bf16[64,1,2,16,256]{4,3,2,1,0:T(8,128)(2,1)}), bf16[64,1,2,16,256]{4,3,2,1,0:T(8,128)(2,1)S(1)}, u32[]{:S(2)}, u32[]{:S(2)}) async-start(bf16[64,1,2,16,256]{4,3,2,1,0:T(8,128)(2,1)} %stack.8), calls=%async_computation.2 | async-start | bytes 2097152 | tf_op jit(solution)/shard_map/all_to_all | solution.py:53
  94.3 50.0 %all-to-all-start = ((bf16[64,1,2,16,256]{4,3,2,1,0:T(8,128)(2,1)}), bf16[64,1,2,16,256]{4,3,2,1,0:T(8,128)(2,1)}, u32[]{:S(2)}, u32[]{:S(2)}) async-start(bf16[64,1,2,16,256]{4,3,2,1,0:T(8,128)(2,1)} %stack.6), calls=%async_computation | async-start | bytes 2097152 | tf_op jit(solution)/shard_map/all_to_all | solution.py:53
  105.7 814.4 %all-reduce.2.cloned.1.call-start = ((), (), s32[]{:S(2)}) async-start(), calls=%async_computation.3 | async-start | bytes 4194304 | tf_op jit(solution)/shard_map/psum | solution.py:64
  175.1 2.2 copy-start.1
  177.3 2.2 copy-start
  180.8 3.7 copy-start.2
Sparse Core Ops, SparseCore 0:
  196.9 723.1 all-reduce.1
